TPU v7x, 32 devices: a whole 2x2x4 slice. The times are simulated.
32 devices in a mesh: mem: 8 (over y, x, core), reg: 4 (over z).
Axes of the slice: x: 2, y: 2, z: 4, core: 2. Of those that a mesh axis runs over, the one named last changes fastest.
Arguments:
- sample_stack: float32 [64, 11, 8, 256], P('mem', None, 'reg'), may hold values from -6 to 6
- weights: float32 [4, 64], P('reg', 'mem'), may hold values from 0.1 to 10
- offspring: int32 [4, 64], P('reg'), may hold values from 0 to 63
- localize: float32 [8, 256], P('reg'), may hold values from 0.2 to 0.9
Outputs:
- posterior: float32 [64, 11, 8, 256], P('mem', None, 'reg')
Inputs may be any that keep to these rules, and one draw needn't show every extreme that they name: `offspring`: each entry names a member.
All inputs are finite; a program needn't handle non-finite values.
Results may differ from a plain program's by a relative error of at most 0.0021.
Values may be sent and summed in bfloat16 or wider, within the bound.
A program may use at most 64 MiB of HBM per device.

v0:
```python
import jax
import jax.numpy as jnp
from jax import lax
from jax.sharding import PartitionSpec as P

wave_gain = 0.25
advect_gain = 0.1
diffuse_gain = 0.1
small_eps = 1e-05


def extended(block, sides, width):
    for axis, dim in sides:
        count = lax.axis_size(axis)
        forward = [(i, i + 1) for i in range(count - 1)]
        forward.append((count - 1, 0))
        backward = [(target, source) for source, target in forward]
        low = lax.ppermute(
            lax.slice_in_dim(block, block.shape[dim] - width, None, axis=dim), axis, forward
        )
        high = lax.ppermute(lax.slice_in_dim(block, 0, width, axis=dim), axis, backward)
        block = jnp.concatenate([low, block, high], axis=dim)
    return block


def advance(padded):
    centre = padded[:, :, 1:-1]
    upper_rows = padded[:, :, 2:]
    lower_rows = padded[:, :, :-2]
    right_cols = jnp.roll(centre, -1, 3)
    left_cols = jnp.roll(centre, 1, 3)
    slope_east = 0.5 * (right_cols - left_cols)
    slope_north = 0.5 * (upper_rows - lower_rows)
    laplace = right_cols + left_cols + upper_rows + lower_rows - 4.0 * centre
    height = centre[:, 0]
    flow_east = centre[:, 1]
    flow_north = centre[:, 2]
    tracer = centre[:, 3:]
    new_height = height - wave_gain * (slope_east[:, 1] + slope_north[:, 2])
    new_east = flow_east - wave_gain * slope_east[:, 0]
    new_north = flow_north - wave_gain * slope_north[:, 0]
    new_tracer = (
        tracer
        - advect_gain
        * (flow_east[:, None] * slope_east[:, 3:] + flow_north[:, None] * slope_north[:, 3:])
        + diffuse_gain * laplace[:, 3:]
    )
    return jnp.concatenate(
        [new_height[:, None], new_east[:, None], new_north[:, None], new_tracer], axis=1
    )


def single_propagation(model_snapshot):
    padded = extended(model_snapshot, (("reg", 2),), 1)
    return advance(padded)


def per_device(sample_stack, weights, offspring, localize):
    sample_collection = sample_stack.shape[0]
    background_prediction = single_propagation(single_propagation(sample_stack))
    importance_factors = weights[0][:, None, None, None]
    total_local = jnp.sum(weights[0])
    zonal_average_vector = jnp.sum(importance_factors * background_prediction, axis=0)
    weight_total, first_sum = lax.psum((total_local, zonal_average_vector), "mem")
    sample_average_map = first_sum / weight_total
    sample_departure = background_prediction - sample_average_map
    variance = (
        lax.psum(jnp.sum(importance_factors * sample_departure * sample_departure, axis=0), "mem")
        / weight_total
    )
    unrolled_lattice = background_prediction.astype(jnp.bfloat16).reshape(sample_collection, -1)
    source_ids = offspring[0]
    member_base = lax.axis_index("mem") * sample_collection
    own_ids = member_base + jnp.arange(sample_collection, dtype=jnp.int32)
    onehot = (source_ids[:, None] == own_ids[None, :]).astype(jnp.bfloat16)
    sample_duplicates = lax.psum_scatter(
        jnp.dot(onehot, unrolled_lattice, preferred_element_type=jnp.float32).astype(jnp.bfloat16),
        "mem",
        scatter_dimension=0,
        tiled=True,
    ).astype(jnp.float32)
    sample_duplicates = sample_duplicates.reshape(background_prediction.shape)
    cell_weight_value = localize[None, None]
    spread_offset = cell_weight_value * (sample_duplicates - sample_average_map) + (
        1.0 - cell_weight_value
    ) * (background_prediction - sample_average_map)
    total_members = sample_collection * lax.axis_size("mem")
    spread = lax.psum(jnp.sum(spread_offset * spread_offset, axis=0), "mem") / total_members
    scale_ratio = jnp.sqrt((variance + small_eps) / (spread + small_eps))
    return sample_average_map + scale_ratio * spread_offset


def solution(mesh):
    in_specs = (P("mem", None, "reg", None), P("reg", "mem"), P("reg", None), P("reg", None))
    out_specs = P("mem", None, "reg", None)
    return jax.shard_map(
        per_device, mesh=mesh, in_specs=in_specs, out_specs=out_specs, check_vma=False
    )
```

profile of v0, /device:TPU:0, one launch (start us, length us, event | category | flops | bytes accessed | tf_op | source)
XLA Modules:
  0.0 99.8 jit_solution(2924346324299373953)
XLA Ops:
  6.5 0.0 copy-start
  6.5 0.0 reduce-scatter.2.cloned.1.call-start
  6.5 1.2 %fusion.51 = (f32[8,11,1,256]{3,2,1,0:T(1,128)S(1)}, f32[8,11,1,256]{3,2,1,0:T(1,128)S(1)}) fusion(f32[8,11,2,256]{3,2,1,0:T(2,128)} %param.4), kind=kLoop, calls=%fused_computation.102 | loop fusion | bytes 360448 | tf_op jit(solution)/shard_map/slice | solution.py:19
  7.8 5.1 %collective-permute-start = (f32[8,11,1,256]{3,2,1,0:T(1,128)S(1)}, f32[8,11,1,256]{3,2,1,0:T(1,128)S(1)}, u32[]{:S(2)}, u32[]{:S(2)}) collective-permute-start(f32[8,11,1,256]{3,2,1,0:T(1,128)S(1)} %get-tuple-element.33), channel_id=1, source_target_pairs={{1,0},{2,1},{3,2},{0,3},{5,4},{6,5},{7,6},{4,7},{9,8},{10,9},{11,1... | collective-permute-start | bytes 270344 | tf_op jit(solution)/shard_map/ppermute | solution.py:21
  12.9 0.0 collective-permute-start.1
  12.9 1.1 %fusion.50 = (f32[8,11,2,1]{3,2,1,0:T(2,128)S(1)}, f32[8,11,2,1]{3,2,1,0:T(2,128)S(1)}) fusion(f32[8,11,2,256]{3,2,1,0:T(2,128)} %param.4), kind=kLoop, calls=%fused_computation.101 | loop fusion | bytes 2816 | tf_op jit(solution)/shard_map/jit(_roll_static)/slice | solution.py:30
  14.0 0.0 copy-done
  14.0 0.3 fusion.49
  14.2 0.4 fusion.3
  14.6 1.1 %collective-permute-done = f32[8,11,1,256]{3,2,1,0:T(1,128)S(1)} collective-permute-done((f32[8,11,1,256]{3,2,1,0:T(1,128)S(1)}, f32[8,11,1,256]{3,2,1,0:T(1,128)S(1)}, u32[]{:S(2)}, u32[]{:S(2)}) %collective-permute-start) | collective-permute-done | bytes 90144 | tf_op jit(solution)/shard_map/ppermute | solution.py:21
  15.7 3.5 %collective-permute-done.1 = f32[8,11,1,256]{3,2,1,0:T(1,128)S(1)} collective-permute-done((f32[8,11,1,256]{3,2,1,0:T(1,128)S(1)}, f32[8,11,1,256]{3,2,1,0:T(1,128)S(1)}, u32[]{:S(2)}, u32[]{:S(2)}) %collective-permute-start.1) | collective-permute-done | bytes 90144 | tf_op jit(solution)/shard_map/ppermute | solution.py:18
  19.2 0.3 fusion.5
  19.6 0.6 fusion.32
  20.2 0.1 pad_maximum_fusion.14
  20.3 0.1 fusion.48
  20.4 0.2 fusion.47
  20.6 0.3 fusion.46
  20.8 0.1 collective-permute-start.3
  20.9 3.8 %collective-permute-start.2 = (f32[8,11,1,256]{3,2,1,0:T(1,128)S(1)}, f32[8,11,1,256]{3,2,1,0:T(1,128)S(1)}, u32[]{:S(2)}, u32[]{:S(2)}) collective-permute-start(f32[8,11,1,256]{3,2,1,0:T(1,128)S(1)} %get-tuple-element.24), channel_id=1, source_target_pairs={{1,0},{2,1},{3,2},{0,3},{5,4},{6,5},{7,6},{4,7},{9,8},{10,9},{11,1... | collective-permute-start | bytes 270344 | tf_op jit(solution)/shard_map/ppermute | solution.py:21
  24.7 0.4 fusion.1
  25.1 2.1 %collective-permute-done.3 = f32[8,11,1,256]{3,2,1,0:T(1,128)S(1)} collective-permute-done((f32[8,11,1,256]{3,2,1,0:T(1,128)S(1)}, f32[8,11,1,256]{3,2,1,0:T(1,128)S(1)}, u32[]{:S(2)}, u32[]{:S(2)}) %collective-permute-start.3) | collective-permute-done | bytes 90144 | tf_op jit(solution)/shard_map/ppermute | solution.py:18
  27.2 0.0 collective-permute-done.2
  27.2 0.4 subtract_multiply_fusion
  27.6 0.0 copy-start.2
  27.6 0.4 fusion.25
  28.1 0.0 copy-start.3
  28.1 0.2 copy-done.2
  28.3 0.2 multiply_reduce_fusion.1
  28.5 0.1 concatenate.46
  28.6 0.1 copy-done.3
  28.7 0.0 copy-start.1
  28.7 1.2 %convolution_convert_fusion = bf16[64,5632]{1,0:T(8,128)(2,1)} fusion(f32[8,5632]{1,0:T(8,128)S(1)} %concatenate.46, s32[8]{0:T(128)S(1)} %iota_add_fusion, s32[64]{0:T(128)S(1)} %bitcast.21), kind=kOutput, calls=%fused_computation | convolution fusion | flops 6173184 | bytes 901408 | tf_op jit(solution)/shard_map/dot_general | solution.py:77
  30.0 0.0 reduce-scatter.2.cloned.1.call-update
  30.0 0.0 copy-done.1
  30.1 0.6 reduce_sum.39
  30.7 23.4 %all-reduce.1 = (f32[11,2,256]{2,1,0:T(2,128)S(1)}, f32[]{:T(128)}) all-reduce(f32[11,2,256]{2,1,0:T(2,128)S(1)} %get-tuple-element.9, f32[]{:T(128)} %reduce_sum.39), channel_id=1, replica_groups=mesh['mem'=8,'reg'=4] {'mem'}, use_global_device_ids=true, to_apply=%region_1.2 | all-reduce | flops 5633 | bytes 45064 | tf_op jit(solution)/shard_map/psum | solution.py:64
  54.1 0.7 broadcast_divide_fusion
  54.8 0.2 fusion.6
  55.0 11.4 %reduce-scatter.2.cloned.1.call-done = bf16[8,5632]{1,0:T(8,128)(2,1)} async-done(((bf16[64,5632]{1,0:T(8,128)(2,1)}), bf16[8,5632]{1,0:T(8,128)(2,1)}) %reduce-scatter.2.cloned.1.call-update) | async-done | bytes 90128 | tf_op jit(solution)/shard_map/reduce_scatter | solution.py:76
  66.4 0.9 convert
  67.3 1.0 multiply_reduce_fusion
  68.3 23.1 %all-reduce = (f32[11,2,256]{2,1,0:T(2,128)S(1)}, f32[11,2,256]{2,1,0:T(2,128)S(1)}) all-reduce(f32[11,2,256]{2,1,0:T(2,128)S(1)} %reduce_sum.42, f32[11,2,256]{2,1,0:T(2,128)S(1)} %fusion.6), channel_id=1, replica_groups=mesh['mem'=8,'reg'=4] {'mem'}, use_global_device_ids=true, to_apply=%region_8.9 | all-reduce | flops 11264 | bytes 90112 | tf_op jit(solution)/shard_map/psum | solution.py:88
  91.4 0.7 fusion.35
  92.1 0.8 fusion.10
  (10 shorter events, 0.2 us)
Async XLA Ops:
  6.5 7.4 %copy-start = (f32[8,11,2,256]{3,2,1,0:T(2,128)S(1)}, f32[8,11,2,256]{3,2,1,0:T(2,128)}, u32[]{:S(2)}) copy-start(f32[8,11,2,256]{3,2,1,0:T(2,128)} %param.4) | copy-start | bytes 540676
  6.5 59.8 %reduce-scatter.2.cloned.1.call-start = ((), (), s32[]{:S(2)}) async-start(), calls=%async_computation.1 | async-start | bytes 811008 | tf_op jit(solution)/shard_map/reduce_scatter | solution.py:76
  7.8 7.9 %collective-permute-start = (f32[8,11,1,256]{3,2,1,0:T(1,128)S(1)}, f32[8,11,1,256]{3,2,1,0:T(1,128)S(1)}, u32[]{:S(2)}, u32[]{:S(2)}) collective-permute-start(f32[8,11,1,256]{3,2,1,0:T(1,128)S(1)} %get-tuple-element.33), channel_id=1, source_target_pairs={{1,0},{2,1},{3,2},{0,3},{5,4},{6,5},{7,6},{4,7},{9,8},{10,9},{11,1... | collective-permute-start | bytes 270344 | tf_op jit(solution)/shard_map/ppermute | solution.py:21
  12.9 6.3 %collective-permute-start.1 = (f32[8,11,1,256]{3,2,1,0:T(1,128)S(1)}, f32[8,11,1,256]{3,2,1,0:T(1,128)S(1)}, u32[]{:S(2)}, u32[]{:S(2)}) collective-permute-start(f32[8,11,1,256]{3,2,1,0:T(1,128)S(1)} %get-tuple-element.32), channel_id=1, source_target_pairs={{0,1},{1,2},{2,3},{3,0},{4,5},{5,6},{6,7},{7,4},{8,9},{9,10},{10,1... | collective-permute-start | bytes 270344 | tf_op jit(solution)/shard_map/ppermute | solution.py:18
  20.8 6.4 %collective-permute-start.3 = (f32[8,11,1,256]{3,2,1,0:T(1,128)S(1)}, f32[8,11,1,256]{3,2,1,0:T(1,128)S(1)}, u32[]{:S(2)}, u32[]{:S(2)}) collective-permute-start(f32[8,11,1,256]{3,2,1,0:T(1,128)S(1)} %get-tuple-element.25), channel_id=1, source_target_pairs={{0,1},{1,2},{2,3},{3,0},{4,5},{5,6},{6,7},{7,4},{8,9},{9,10},{10,1... | collective-permute-start | bytes 270344 | tf_op jit(solution)/shard_map/ppermute | solution.py:18
  20.9 6.3 %collective-permute-start.2 = (f32[8,11,1,256]{3,2,1,0:T(1,128)S(1)}, f32[8,11,1,256]{3,2,1,0:T(1,128)S(1)}, u32[]{:S(2)}, u32[]{:S(2)}) collective-permute-start(f32[8,11,1,256]{3,2,1,0:T(1,128)S(1)} %get-tuple-element.24), channel_id=1, source_target_pairs={{1,0},{2,1},{3,2},{0,3},{5,4},{6,5},{7,6},{4,7},{9,8},{10,9},{11,1... | collective-permute-start | bytes 270344 | tf_op jit(solution)/shard_map/ppermute | solution.py:21
  27.6 0.7 copy-start.2
  28.1 0.7 copy-start.3
  28.7 1.3 %copy-start.1 = (f32[2,256]{1,0:T(2,128)S(1)}, f32[2,256]{1,0:T(2,128)}, u32[]{:S(2)}) copy-start(f32[2,256]{1,0:T(2,128)} %param.7) | copy-start | bytes 6148
Sparse Core Ops, SparseCore 0:
  30.1 36.2 reduce-scatter.1
where the time goes:
time: 100 us; the launch traced here: 99.8 us
  blocking collectives  46.5 us (46%)
  waiting for transfers between devices  18.1 us (18%)
  between operations  13.6 us (14%)
  starting transfers between devices  8.97 us (9%)
  other arithmetic  7.64 us (8%)
  local copies, waits for them, and re-layouts  3.69 us (4%)
  matrix products  1.24 us (1%)
    psum x1, blocking collectives, per_device(): lax.psum((total_local, zonal_average_vector), 'mem')  23.4 us
    psum x1, blocking collectives, per_device(): lax.psum(jnp.sum(spread_offset * spread_offset, axis=0), 'mem')  23.1 us
    reduce_scatter x1, waiting for transfers between devices, per_device(): lax.psum_scatter(jnp.dot(onehot, unrolled_lattice, preferred_element_type...  11.4 us
    ppermute x2, starting transfers between devices, extended(): lax.ppermute(lax.slice_in_dim(block, 0, width, axis=dim), axis, backward)  8.91 us
    ppermute x2, waiting for transfers between devices, extended(): lax.ppermute(lax.slice_in_dim(block, block.shape[dim] - width, None, axis...  5.62 us
  transfers between devices with their start and end apart: 5, of which 4 were waited for; matrix products, arithmetic and copies ran while one was open for 4% of the time, Pallas kernels for 0%

commit v1 on v0

--- a/solution.py
+++ b/solution.py
@@ -85,7 +85,10 @@
         1.0 - cell_weight_value
     ) * (background_prediction - sample_average_map)
     total_members = sample_collection * lax.axis_size("mem")
-    spread = lax.psum(jnp.sum(spread_offset * spread_offset, axis=0), "mem") / total_members
+    spread = (
+        jnp.sum(lax.all_gather(jnp.sum(spread_offset * spread_offset, axis=0), "mem"), axis=0)
+        / total_members
+    )
     scale_ratio = jnp.sqrt((variance + small_eps) / (spread + small_eps))
     return sample_average_map + scale_ratio * spread_offset
 

time: 100 us -> 96.5 us (0.965)
  waiting for transfers between devices: 18.1 us -> 6.75 us
  blocking collectives: 46.5 us -> 54.2 us
    reduce_scatter x1, waiting for transfers between devices: 11.4 us -> 0.01 us  [per_device(): lax.psum_scatter(jnp.dot(onehot, unrolled_lattice, preferred_element_type...]
    all_gather x0 -> x1, blocking collectives: none -> 8.31 us  [per_device(): lax.all_gather(jnp.sum(spread_offset * spread_offset, axis=0), 'mem')]
  transfers between devices with their start and end apart: 5 -> 5, of which waited for: 4 -> 3; matrix products, arithmetic and copies ran while one was open for 4% -> 4% of each run, Pallas kernels for 0% -> 0%
where the time goes in v1:
time: 96.5 us; the launch traced here: 96.1 us
  blocking collectives  54.2 us (56%)
  between operations  13.6 us (14%)
  starting transfers between devices  8.97 us (9%)
  other arithmetic  7.7 us (8%)
  waiting for transfers between devices  6.75 us (7%)
  local copies, waits for them, and re-layouts  3.69 us (4%)
  matrix products  1.24 us (1%)
    psum x1, blocking collectives, per_device(): lax.psum((total_local, zonal_average_vector), 'mem')  23.4 us
    psum x1, blocking collectives, per_device(): lax.psum(jnp.sum(importance_factors * sample_departure * sample_departure...  22.5 us
    ppermute x2, starting transfers between devices, extended(): lax.ppermute(lax.slice_in_dim(block, 0, width, axis=dim), axis, backward)  8.91 us
    all_gather x1, blocking collectives, per_device(): lax.all_gather(jnp.sum(spread_offset * spread_offset, axis=0), 'mem')  8.31 us
    ppermute x2, waiting for transfers between devices, extended(): lax.ppermute(lax.slice_in_dim(block, block.shape[dim] - width, None, axis...  5.62 us
  transfers between devices with their start and end apart: 5, of which 3 were waited for; matrix products, arithmetic and copies ran while one was open for 4% of the time, Pallas kernels for 0%

profile of v1, /device:TPU:0, one launch (start us, length us, event | category | flops | bytes accessed | tf_op | source)
XLA Modules:
  0.0 96.1 jit_solution(10966484264766346778)
XLA Ops:
  6.5 0.0 copy-start
  6.5 0.0 reduce-scatter.2.cloned.1.call-start
  6.5 1.2 %fusion.51 = (f32[8,11,1,256]{3,2,1,0:T(1,128)S(1)}, f32[8,11,1,256]{3,2,1,0:T(1,128)S(1)}) fusion(f32[8,11,2,256]{3,2,1,0:T(2,128)} %param.4), kind=kLoop, calls=%fused_computation.102 | loop fusion | bytes 360448 | tf_op jit(solution)/shard_map/slice | solution.py:19
  7.8 5.1 %collective-permute-start = (f32[8,11,1,256]{3,2,1,0:T(1,128)S(1)}, f32[8,11,1,256]{3,2,1,0:T(1,128)S(1)}, u32[]{:S(2)}, u32[]{:S(2)}) collective-permute-start(f32[8,11,1,256]{3,2,1,0:T(1,128)S(1)} %get-tuple-element.31), channel_id=1, source_target_pairs={{1,0},{2,1},{3,2},{0,3},{5,4},{6,5},{7,6},{4,7},{9,8},{10,9},{11,1... | collective-permute-start | bytes 270344 | tf_op jit(solution)/shard_map/ppermute | solution.py:21
  12.9 0.0 collective-permute-start.1
  12.9 1.1 %fusion.50 = (f32[8,11,2,1]{3,2,1,0:T(2,128)S(1)}, f32[8,11,2,1]{3,2,1,0:T(2,128)S(1)}) fusion(f32[8,11,2,256]{3,2,1,0:T(2,128)} %param.4), kind=kLoop, calls=%fused_computation.101 | loop fusion | bytes 2816 | tf_op jit(solution)/shard_map/jit(_roll_static)/slice | solution.py:30
  14.0 0.0 copy-done
  14.0 0.3 fusion.49
  14.2 0.4 fusion.3
  14.6 1.1 %collective-permute-done = f32[8,11,1,256]{3,2,1,0:T(1,128)S(1)} collective-permute-done((f32[8,11,1,256]{3,2,1,0:T(1,128)S(1)}, f32[8,11,1,256]{3,2,1,0:T(1,128)S(1)}, u32[]{:S(2)}, u32[]{:S(2)}) %collective-permute-start) | collective-permute-done | bytes 90144 | tf_op jit(solution)/shard_map/ppermute | solution.py:21
  15.7 3.5 %collective-permute-done.1 = f32[8,11,1,256]{3,2,1,0:T(1,128)S(1)} collective-permute-done((f32[8,11,1,256]{3,2,1,0:T(1,128)S(1)}, f32[8,11,1,256]{3,2,1,0:T(1,128)S(1)}, u32[]{:S(2)}, u32[]{:S(2)}) %collective-permute-start.1) | collective-permute-done | bytes 90144 | tf_op jit(solution)/shard_map/ppermute | solution.py:18
  19.2 0.3 fusion.5
  19.6 0.6 fusion.32
  20.2 0.1 pad_maximum_fusion.14
  20.3 0.1 fusion.48
  20.4 0.2 fusion.47
  20.6 0.3 fusion.46
  20.8 0.1 collective-permute-start.3
  20.9 3.8 %collective-permute-start.2 = (f32[8,11,1,256]{3,2,1,0:T(1,128)S(1)}, f32[8,11,1,256]{3,2,1,0:T(1,128)S(1)}, u32[]{:S(2)}, u32[]{:S(2)}) collective-permute-start(f32[8,11,1,256]{3,2,1,0:T(1,128)S(1)} %get-tuple-element.22), channel_id=1, source_target_pairs={{1,0},{2,1},{3,2},{0,3},{5,4},{6,5},{7,6},{4,7},{9,8},{10,9},{11,1... | collective-permute-start | bytes 270344 | tf_op jit(solution)/shard_map/ppermute | solution.py:21
  24.7 0.4 fusion.1
  25.1 2.1 %collective-permute-done.3 = f32[8,11,1,256]{3,2,1,0:T(1,128)S(1)} collective-permute-done((f32[8,11,1,256]{3,2,1,0:T(1,128)S(1)}, f32[8,11,1,256]{3,2,1,0:T(1,128)S(1)}, u32[]{:S(2)}, u32[]{:S(2)}) %collective-permute-start.3) | collective-permute-done | bytes 90144 | tf_op jit(solution)/shard_map/ppermute | solution.py:18
  27.2 0.0 collective-permute-done.2
  27.2 0.4 subtract_multiply_fusion
  27.6 0.0 copy-start.2
  27.6 0.4 fusion.25
  28.1 0.0 copy-start.3
  28.1 0.2 copy-done.2
  28.3 0.2 multiply_reduce_fusion.1
  28.5 0.1 concatenate.46
  28.6 0.1 copy-done.3
  28.7 0.0 copy-start.1
  28.7 1.2 %convolution_convert_fusion = bf16[64,5632]{1,0:T(8,128)(2,1)} fusion(f32[8,5632]{1,0:T(8,128)S(1)} %concatenate.46, s32[8]{0:T(128)S(1)} %iota_add_fusion, s32[64]{0:T(128)S(1)} %bitcast.21), kind=kOutput, calls=%fused_computation | convolution fusion | flops 6173184 | bytes 901408 | tf_op jit(solution)/shard_map/dot_general | solution.py:77
  30.0 0.0 reduce-scatter.2.cloned.1.call-update
  30.0 0.0 copy-done.1
  30.1 0.6 reduce_sum.46
  30.7 23.4 %all-reduce = (f32[11,2,256]{2,1,0:T(2,128)S(1)}, f32[]{:T(128)}) all-reduce(f32[11,2,256]{2,1,0:T(2,128)S(1)} %get-tuple-element.7, f32[]{:T(128)} %reduce_sum.46), channel_id=1, replica_groups=mesh['mem'=8,'reg'=4] {'mem'}, use_global_device_ids=true, to_apply=%region_1.2 | all-reduce | flops 5633 | bytes 45064 | tf_op jit(solution)/shard_map/psum | solution.py:64
  54.1 0.7 broadcast_divide_fusion
  54.8 0.2 fusion.6
  55.0 22.5 %psum.23 = f32[11,2,256]{2,1,0:T(2,128)S(1)} all-reduce(f32[11,2,256]{2,1,0:T(2,128)S(1)} %fusion.6), channel_id=1, replica_groups=mesh['mem'=8,'reg'=4] {'mem'}, use_global_device_ids=true, to_apply=%region_5.6 | all-reduce | flops 5632 | bytes 45056 | tf_op jit(solution)/shard_map/psum | solution.py:68
  77.4 0.0 reduce-scatter.2.cloned.1.call-done
  77.4 0.9 convert
  78.3 1.0 %multiply_reduce_fusion = f32[5632]{0:T(1024)S(1)} fusion(f32[8,5632]{1,0:T(8,128)S(1)} %concatenate.46, f32[5632]{0:T(1024)S(1)} %mul.204, f32[5632]{0:T(1024)S(1)} %add.97, f32[5632]{0:T(1024)S(1)} %mul.199, bf16[8,5632]{1,0:T(8,128)(2,1)} %reduce-scatter.2.cloned.1.call-done), kind=kLoop, calls=%fused_computation.35 | loop fusion | flops 354816 | bytes 360448 | tf_op jit(solution)/shard_map/reduce_sum | solution.py:89
  79.4 8.3 %all_gather.7 = f32[8,11,2,256]{3,2,1,0:T(2,128)S(1)} all-gather(f32[1,11,2,256]{3,2,1,0:T(2,128)S(1)} %all_gather.6), channel_id=1, replica_groups=mesh['mem'=8,'reg'=4] {'mem'}, dimensions={0}, use_global_device_ids=true | all-gather | bytes 202752 | tf_op jit(solution)/shard_map/all_gather | solution.py:89
  87.7 0.1 reduce_sum.49
  87.7 0.7 fusion.35
  88.4 0.8 fusion.10
  (10 shorter events, 0.2 us)
Async XLA Ops:
  6.5 7.4 %copy-start = (f32[8,11,2,256]{3,2,1,0:T(2,128)S(1)}, f32[8,11,2,256]{3,2,1,0:T(2,128)}, u32[]{:S(2)}) copy-start(f32[8,11,2,256]{3,2,1,0:T(2,128)} %param.4) | copy-start | bytes 540676
  6.5 70.9 %reduce-scatter.2.cloned.1.call-start = ((), (), s32[]{:S(2)}) async-start(), calls=%async_computation.1 | async-start | bytes 811008 | tf_op jit(solution)/shard_map/reduce_scatter | solution.py:76
  7.8 7.9 %collective-permute-start = (f32[8,11,1,256]{3,2,1,0:T(1,128)S(1)}, f32[8,11,1,256]{3,2,1,0:T(1,128)S(1)}, u32[]{:S(2)}, u32[]{:S(2)}) collective-permute-start(f32[8,11,1,256]{3,2,1,0:T(1,128)S(1)} %get-tuple-element.31), channel_id=1, source_target_pairs={{1,0},{2,1},{3,2},{0,3},{5,4},{6,5},{7,6},{4,7},{9,8},{10,9},{11,1... | collective-permute-start | bytes 270344 | tf_op jit(solution)/shard_map/ppermute | solution.py:21
  12.9 6.3 %collective-permute-start.1 = (f32[8,11,1,256]{3,2,1,0:T(1,128)S(1)}, f32[8,11,1,256]{3,2,1,0:T(1,128)S(1)}, u32[]{:S(2)}, u32[]{:S(2)}) collective-permute-start(f32[8,11,1,256]{3,2,1,0:T(1,128)S(1)} %get-tuple-element.30), channel_id=1, source_target_pairs={{0,1},{1,2},{2,3},{3,0},{4,5},{5,6},{6,7},{7,4},{8,9},{9,10},{10,1... | collective-permute-start | bytes 270344 | tf_op jit(solution)/shard_map/ppermute | solution.py:18
  20.8 6.4 %collective-permute-start.3 = (f32[8,11,1,256]{3,2,1,0:T(1,128)S(1)}, f32[8,11,1,256]{3,2,1,0:T(1,128)S(1)}, u32[]{:S(2)}, u32[]{:S(2)}) collective-permute-start(f32[8,11,1,256]{3,2,1,0:T(1,128)S(1)} %get-tuple-element.23), channel_id=1, source_target_pairs={{0,1},{1,2},{2,3},{3,0},{4,5},{5,6},{6,7},{7,4},{8,9},{9,10},{10,1... | collective-permute-start | bytes 270344 | tf_op jit(solution)/shard_map/ppermute | solution.py:18
  20.9 6.3 %collective-permute-start.2 = (f32[8,11,1,256]{3,2,1,0:T(1,128)S(1)}, f32[8,11,1,256]{3,2,1,0:T(1,128)S(1)}, u32[]{:S(2)}, u32[]{:S(2)}) collective-permute-start(f32[8,11,1,256]{3,2,1,0:T(1,128)S(1)} %get-tuple-element.22), channel_id=1, source_target_pairs={{1,0},{2,1},{3,2},{0,3},{5,4},{6,5},{7,6},{4,7},{9,8},{10,9},{11,1... | collective-permute-start | bytes 270344 | tf_op jit(solution)/shard_map/ppermute | solution.py:21
  27.6 0.7 copy-start.2
  28.1 0.7 copy-start.3
  28.7 1.3 %copy-start.1 = (f32[2,256]{1,0:T(2,128)S(1)}, f32[2,256]{1,0:T(2,128)}, u32[]{:S(2)}) copy-start(f32[2,256]{1,0:T(2,128)} %param.7) | copy-start | bytes 6148
Sparse Core Ops, SparseCore 0:
  30.1 36.2 reduce-scatter.1
